TPU v7x, 32 devices: a whole 2x2x4 slice. The times are simulated.
32 devices in a mesh: dp: 16 (over z, y, x), seq: 2 (over core).
Axes of the slice: x: 2, y: 2, z: 4, core: 2. Of those that a mesh axis runs over, the one named last changes fastest.
Arguments:
- latents: float32 [16, 256, 48], P('dp', 'seq'), may hold values from -6 to 6
- valid: int32 [16, 256], P('dp', 'seq'), may hold values 0 or 1
- class_labels: int32 [16], replicated, may hold values from 0 to 447
- group_perm: int32 [16], P('dp'), may hold values from 0 to 15, as said below
- patch_weight: bfloat16 [48, 768], replicated, may hold values from -0.875 to 0.875
- pos_table: bfloat16 [256, 768], P('seq'), may hold values from -3 to 3
- class_table: bfloat16 [1024, 768], replicated, may hold values from -3 to 3
- ln1_gain: bfloat16 [1, 768], replicated, may hold values from 0.25 to 1.75
- ln1_bias: bfloat16 [1, 768], replicated, may hold values from -1.5 to 1.5
- qkv_weight: bfloat16 [1, 768, 2304], replicated, may hold values from -0.21875 to 0.21875
- out_weight: bfloat16 [1, 768, 768], replicated, may hold values from -0.875 to 0.875
- ln2_gain: bfloat16 [1, 768], replicated, may hold values from 0.25 to 1.75
- ln2_bias: bfloat16 [1, 768], replicated, may hold values from -1.5 to 1.5
- up_weight: bfloat16 [1, 768, 3072], replicated, may hold values from -0.21875 to 0.21875
- up_bias: bfloat16 [1, 3072], replicated, may hold values from -1.5 to 1.5
- down_weight: bfloat16 [1, 3072, 768], replicated, may hold values from -0.109375 to 0.109375
- head_weight: bfloat16 [768, 96], replicated, may hold values from -0.109375 to 0.109375
- head_bias: bfloat16 [96], replicated, may hold values from -1 to 1
- cot_latents: float32 [16, 256, 48], P('dp', 'seq'), may hold values from -6 to 6
- cot_logdet: float32 [16], P('dp'), may hold values from -4 to 4
Outputs:
- new_latents: float32 [16, 256, 48], P('dp', 'seq')
- logdet: float32 [16], P('dp')
- latents_grad: float32 [16, 256, 48], P('dp', 'seq')
- patch_weight_grad: float32 [48, 768], replicated
- pos_grad: float32 [256, 768], P('seq')
- class_grad: float32 [1024, 768], P('dp')
- ln1_gain_grad: float32 [1, 768], replicated
- ln1_bias_grad: float32 [1, 768], replicated
- qkv_grad: float32 [1, 768, 2304], replicated
- out_grad: float32 [1, 768, 768], replicated
- ln2_gain_grad: float32 [1, 768], replicated
- ln2_bias_grad: float32 [1, 768], replicated
- up_grad: float32 [1, 768, 3072], replicated
- up_bias_grad: float32 [1, 3072], replicated
- down_grad: float32 [1, 3072, 768], replicated
- head_weight_grad: float32 [768, 96], replicated
- head_bias_grad: float32 [96], replicated
Inputs may be any that keep to these rules, and one draw needn't show every extreme that they name: Each of 0 to 15 once; class_labels[group_perm] never falls.
All inputs are finite; a program needn't handle non-finite values. No bound on the sum of `valid` on one device may be relied on, other than what follows from the above.
Results may differ from a plain program's by a relative error of at most 0.023.
Values may be sent and summed in bfloat16 or wider, within the bound.
A program may use at most 320 MiB of HBM per device.

v0:
```python
import jax
import jax.numpy as jnp
from jax import lax
from jax.sharding import PartitionSpec as P

HEAD_DIM = 64
precise = lax.Precision.HIGHEST
norm_eps = 1e-05


def shifted_2(shard, axis, by):
    size = lax.axis_size(axis)
    pairs = [(i, i + by) for i in range(size) if 0 <= i + by < size]
    return lax.ppermute(shard, axis, pairs)


def layer_norm(values, norm_gain, norm_bias):
    center = values - jnp.mean(values, -1, keepdims=True)
    spread = jnp.mean(center * center, -1, keepdims=True)
    return center * lax.rsqrt(spread + norm_eps) * norm_gain + norm_bias


def matmul(left_side, weight_mat):
    return jnp.dot(left_side, weight_mat, preferred_element_type=jnp.float32)


def outer_sum(left_side, grad_side):
    left_flat = left_side.reshape(-1, left_side.shape[-1])
    grad_flat = grad_side.reshape(-1, grad_side.shape[-1])
    return lax.dot_general(
        left_flat, grad_flat, (((0,), (0,)), ((), ())), preferred_element_type=jnp.float32
    )


def transposed(grad_side, weight_mat):
    return lax.dot_general(
        grad_side,
        weight_mat,
        (((grad_side.ndim - 1,), (1,)), ((), ())),
        preferred_element_type=jnp.float32,
    )


def eight_rows(matrix):
    return matrix.reshape(8, -1)


def attention_mask(key_valid, patch_rows, seq_place):
    query_pos = seq_place * patch_rows + lax.iota(jnp.int32, patch_rows)
    key_pos = (seq_place - 1) * patch_rows + lax.iota(jnp.int32, 2 * patch_rows)
    earlier = (key_pos[None, :] < query_pos[:, None])[None] & (key_valid[:, None, :] > 0)
    return earlier | (key_pos[None, :] == query_pos[:, None])[None]


def masked_scores(query, keys, allowed):
    logits = jnp.einsum(
        "bqhd,bkhd->bhqk", query, keys, preferred_element_type=jnp.float32
    ) * HEAD_DIM ** (-0.5)
    return jnp.where(allowed[:, None], logits, -1e30)


def forward(latents, valid, class_rows, seq_place, weights):
    (
        patch_weight,
        pos_table,
        qkv_weight,
        out_weight,
        ln1_gain,
        ln1_bias,
        ln2_gain,
        ln2_bias,
        up_weight,
        up_bias,
        down_weight,
        head_weight,
        head_bias,
    ) = weights
    images, patch_rows, channels = latents.shape
    model_width = qkv_weight.shape[1]
    head_count = model_width // HEAD_DIM
    latent_low = latents.astype(jnp.bfloat16)
    hidden = (
        matmul(latent_low, patch_weight)
        + pos_table.astype(jnp.float32)[None]
        + class_rows[:, None, :]
    )
    own_mask = valid.astype(jnp.bfloat16)
    normed = layer_norm(
        hidden, ln1_gain[0].astype(jnp.float32), ln1_bias[0].astype(jnp.float32)
    ).astype(jnp.bfloat16)
    packed = matmul(normed, qkv_weight[0]).astype(jnp.bfloat16)
    query = packed[..., :model_width].reshape(images, patch_rows, head_count, HEAD_DIM)
    keys_own = packed[..., model_width : 2 * model_width]
    values_own = packed[..., 2 * model_width :]
    prior_keys, prior_values, prior_mask = shifted_2((keys_own, values_own, own_mask), "seq", 1)
    keys = jnp.concatenate((prior_keys, keys_own), 1).reshape(
        images, 2 * patch_rows, head_count, HEAD_DIM
    )
    values = jnp.concatenate((prior_values, values_own), 1).reshape(
        images, 2 * patch_rows, head_count, HEAD_DIM
    )
    allowed = attention_mask(jnp.concatenate((prior_mask, own_mask), 1), patch_rows, seq_place)
    logits = masked_scores(query, keys, allowed)
    row_peak = jnp.max(logits, -1, keepdims=True)
    log_total = row_peak + jnp.log(jnp.sum(jnp.exp(logits - row_peak), -1, keepdims=True))
    weights_soft = jnp.exp(logits - log_total).astype(jnp.bfloat16)
    attended = jnp.einsum(
        "bhqk,bkhd->bqhd", weights_soft, values, preferred_element_type=jnp.float32
    )
    attended = attended.astype(jnp.bfloat16).reshape(images, patch_rows, model_width)
    mid = hidden + matmul(attended, out_weight[0])
    second = layer_norm(
        mid, ln2_gain[0].astype(jnp.float32), ln2_bias[0].astype(jnp.float32)
    ).astype(jnp.bfloat16)
    preact = matmul(second, up_weight[0]) + up_bias[0].astype(jnp.float32)
    activated = jax.nn.gelu(preact, approximate=True).astype(jnp.bfloat16)
    saved = [
        (
            hidden,
            normed,
            query,
            keys,
            values,
            allowed,
            log_total,
            attended,
            mid,
            second,
            preact,
            activated,
        )
    ]
    hidden = mid + matmul(activated, down_weight[0])
    top_low = hidden.astype(jnp.bfloat16)
    head_out = matmul(top_low, head_weight) + head_bias.astype(jnp.float32)
    prior_row = shifted_2(head_out[:, patch_rows - 1, :], "seq", 1)
    shifted = jnp.concatenate((prior_row[:, None, :], head_out[:, : patch_rows - 1, :]), 1)
    shifted = shifted * valid.astype(jnp.float32)[..., None]
    alpha = shifted[..., :channels]
    shift_mean = shifted[..., channels:]
    factor = jnp.exp(-alpha)
    new_latents = (latents - shift_mean) * factor
    logdet_part = -jnp.sum(alpha, (1, 2))
    return (new_latents, logdet_part, factor, top_low, saved)


def local(
    latents,
    valid,
    class_labels,
    group_perm,
    patch_weight,
    pos_table,
    class_table,
    ln1_gain,
    ln1_bias,
    qkv_weight,
    out_weight,
    ln2_gain,
    ln2_bias,
    up_weight,
    up_bias,
    down_weight,
    head_weight,
    head_bias,
    cot_latents,
    cot_logdet,
):
    images, patch_rows, channels = latents.shape
    model_width = qkv_weight.shape[1]
    head_count = model_width // HEAD_DIM
    layer_total = qkv_weight.shape[0]
    seq_place = lax.axis_index("seq")
    picks = group_perm[:, None] == lax.iota(jnp.int32, class_labels.shape[0])[None, :]
    image_labels = jnp.sum(jnp.where(picks, class_labels[None, :], 0), 1)
    label_hot = image_labels[:, None] == lax.iota(jnp.int32, class_table.shape[0])[None, :]
    class_rows = matmul(label_hot.astype(jnp.bfloat16), class_table)
    weights = (
        patch_weight,
        pos_table,
        qkv_weight,
        out_weight,
        ln1_gain,
        ln1_bias,
        ln2_gain,
        ln2_bias,
        up_weight,
        up_bias,
        down_weight,
        head_weight,
        head_bias,
    )
    new_latents, logdet_part, factor, top_low, saved = forward(
        latents, valid, class_rows, seq_place, weights
    )
    latents_again, unused = lax.optimization_barrier((latents, new_latents))
    unused_a, unused_b, unused_c, unused_d, saved = forward(
        latents_again, valid, class_rows, seq_place, weights
    )
    valid_float = valid.astype(jnp.float32)
    d_alpha = -cot_latents * new_latents - cot_logdet[:, None, None]
    d_mean = -cot_latents * factor
    d_shifted = jnp.concatenate((d_alpha, d_mean), -1) * valid_float[..., None]
    next_row = shifted_2(d_shifted[:, 0, :], "seq", -1)
    d_head = jnp.concatenate((d_shifted[:, 1:, :], next_row[:, None, :]), 1).astype(jnp.bfloat16)
    head_weight_grad = outer_sum(top_low, d_head)
    head_bias_grad = jnp.sum(d_head.astype(jnp.float32), (0, 1))
    d_hidden = transposed(d_head, head_weight)
    grads_qkv, grads_out, grads_up, grads_down = ([], [], [], [])
    grads_g1, grads_b1, grads_g2, grads_b2, grads_ub = ([], [], [], [], [])
    for layer_index in reversed(range(layer_total)):
        (
            hidden,
            normed,
            query,
            keys,
            values,
            allowed,
            log_total,
            attended,
            mid,
            second,
            preact,
            activated,
        ) = saved[layer_index]
        d_down = d_hidden.astype(jnp.bfloat16)
        down_grad = outer_sum(activated, d_down)
        d_act = transposed(d_down, down_weight[layer_index])
        unused_gelu, gelu_pull = jax.vjp(lambda inner: jax.nn.gelu(inner, approximate=True), preact)
        d_pre = gelu_pull(d_act)[0].astype(jnp.bfloat16)
        up_bias_grad = jnp.sum(d_pre.astype(jnp.float32), (0, 1))
        up_grad = outer_sum(second, d_pre)
        d_second = transposed(d_pre, up_weight[layer_index])
        unused_norm, norm_pull = jax.vjp(
            layer_norm,
            mid,
            ln2_gain[layer_index].astype(jnp.float32),
            ln2_bias[layer_index].astype(jnp.float32),
        )
        d_mid_norm, ln2_gain_part, ln2_bias_part = norm_pull(d_second)
        d_mid = d_hidden + d_mid_norm
        d_proj = d_mid.astype(jnp.bfloat16)
        out_grad = outer_sum(attended, d_proj)
        d_attended = transposed(d_proj, out_weight[layer_index]).astype(jnp.bfloat16)
        d_attended = d_attended.reshape(images, patch_rows, head_count, HEAD_DIM)
        logits = masked_scores(query, keys, allowed)
        probs = jnp.exp(logits - log_total)
        d_probs = jnp.einsum(
            "bqhd,bkhd->bhqk", d_attended, values, preferred_element_type=jnp.float32
        )
        d_scores = (probs * (d_probs - jnp.sum(d_probs * probs, -1, keepdims=True))).astype(
            jnp.bfloat16
        )
        d_query = jnp.einsum(
            "bhqk,bkhd->bqhd", d_scores, keys, preferred_element_type=jnp.float32
        ) * HEAD_DIM ** (-0.5)
        d_keys = jnp.einsum(
            "bhqk,bqhd->bkhd", d_scores, query, preferred_element_type=jnp.float32
        ) * HEAD_DIM ** (-0.5)
        d_values = jnp.einsum(
            "bhqk,bqhd->bkhd",
            probs.astype(jnp.bfloat16),
            d_attended,
            preferred_element_type=jnp.float32,
        )
        d_keys = d_keys.reshape(images, 2 * patch_rows, model_width)
        d_values = d_values.reshape(images, 2 * patch_rows, model_width)
        back_keys, back_values = (
            shifted_2(d_keys[:, :patch_rows].astype(jnp.bfloat16), "seq", -1).astype(jnp.float32),
            shifted_2(d_values[:, :patch_rows].astype(jnp.bfloat16), "seq", -1).astype(jnp.float32),
        )
        d_packed = jnp.concatenate(
            (
                d_query.reshape(images, patch_rows, model_width),
                d_keys[:, patch_rows:] + back_keys,
                d_values[:, patch_rows:] + back_values,
            ),
            -1,
        ).astype(jnp.bfloat16)
        qkv_grad = outer_sum(normed, d_packed)
        d_normed = transposed(d_packed, qkv_weight[layer_index])
        unused_norm, norm_pull = jax.vjp(
            layer_norm,
            hidden,
            ln1_gain[layer_index].astype(jnp.float32),
            ln1_bias[layer_index].astype(jnp.float32),
        )
        d_input, ln1_gain_part, ln1_bias_part = norm_pull(d_normed)
        d_hidden = d_mid + d_input
        grads_qkv.insert(0, qkv_grad)
        grads_out.insert(0, out_grad)
        grads_up.insert(0, up_grad)
        grads_down.insert(0, down_grad)
        grads_g1.insert(0, ln1_gain_part)
        grads_b1.insert(0, ln1_bias_part)
        grads_g2.insert(0, ln2_gain_part)
        grads_b2.insert(0, ln2_bias_part)
        grads_ub.insert(0, up_bias_grad)
    d_embed_low = d_hidden.astype(jnp.bfloat16)
    patch_grad_part = outer_sum(latents.astype(jnp.bfloat16), d_embed_low)
    latents_grad = cot_latents * factor + transposed(d_embed_low, patch_weight)
    pos_part = jnp.sum(d_hidden, 0)
    class_part = jnp.sum(d_hidden, 1)
    logdet, class_sums = lax.psum((logdet_part, class_part), "seq")
    class_term = lax.dot_general(
        label_hot.astype(jnp.float32),
        class_sums,
        (((0,), (0,)), ((), ())),
        precision=precise,
        preferred_element_type=jnp.float32,
    )
    class_grad = lax.psum_scatter(class_term, "dp", scatter_dimension=0, tiled=True)
    pos_grad = lax.psum(pos_part, "dp")
    (
        patch_weight_grad,
        head_weight_grad,
        head_bias_grad,
        ln1_gain_grad,
        ln1_bias_grad,
        ln2_gain_grad,
        ln2_bias_grad,
        up_bias_grad,
    ) = lax.psum(
        (
            patch_grad_part,
            head_weight_grad,
            head_bias_grad,
            jnp.stack(grads_g1),
            jnp.stack(grads_b1),
            jnp.stack(grads_g2),
            jnp.stack(grads_b2),
            jnp.stack(grads_ub),
        ),
        ("dp", "seq"),
    )
    qkv_stack = jnp.stack(grads_qkv)
    out_stack = jnp.stack(grads_out)
    up_stack = jnp.stack(grads_up)
    down_stack = jnp.stack(grads_down)
    flat_parts = (
        lax.psum_scatter(eight_rows(qkv_stack), ("dp", "seq"), scatter_dimension=1, tiled=True),
        lax.psum_scatter(eight_rows(out_stack), ("dp", "seq"), scatter_dimension=1, tiled=True),
        lax.psum_scatter(eight_rows(up_stack), ("dp", "seq"), scatter_dimension=1, tiled=True),
        lax.psum_scatter(eight_rows(down_stack), ("dp", "seq"), scatter_dimension=1, tiled=True),
    )
    flat_qkv, flat_out, flat_up, flat_down = (
        lax.all_gather(
            flat_parts[0].astype(jnp.bfloat16), ("dp", "seq"), axis=1, tiled=True
        ).astype(jnp.float32),
        lax.all_gather(
            flat_parts[1].astype(jnp.bfloat16), ("dp", "seq"), axis=1, tiled=True
        ).astype(jnp.float32),
        lax.all_gather(
            flat_parts[2].astype(jnp.bfloat16), ("dp", "seq"), axis=1, tiled=True
        ).astype(jnp.float32),
        lax.all_gather(
            flat_parts[3].astype(jnp.bfloat16), ("dp", "seq"), axis=1, tiled=True
        ).astype(jnp.float32),
    )
    qkv_stack = flat_qkv.reshape(qkv_stack.shape)
    out_stack = flat_out.reshape(out_stack.shape)
    up_stack = flat_up.reshape(up_stack.shape)
    down_stack = flat_down.reshape(down_stack.shape)
    return (
        new_latents,
        logdet,
        latents_grad,
        patch_weight_grad,
        pos_grad,
        class_grad,
        ln1_gain_grad,
        ln1_bias_grad,
        qkv_stack,
        out_stack,
        ln2_gain_grad,
        ln2_bias_grad,
        up_stack,
        up_bias_grad,
        down_stack,
        head_weight_grad,
        head_bias_grad,
    )


def solution(mesh):
    in_specs = (
        P("dp", "seq", None),
        P("dp", "seq"),
        P(),
        P("dp"),
        P(),
        P("seq", None),
        P(),
        P(),
        P(),
        P(),
        P(),
        P(),
        P(),
        P(),
        P(),
        P(),
        P(),
        P(),
        P("dp", "seq", None),
        P("dp"),
    )
    out_specs = (
        P("dp", "seq", None),
        P("dp"),
        P("dp", "seq", None),
        P(),
        P("seq", None),
        P("dp", None),
        P(),
        P(),
        P(),
        P(),
        P(),
        P(),
        P(),
        P(),
        P(),
        P(),
        P(),
    )
    return jax.shard_map(local, mesh=mesh, in_specs=in_specs, out_specs=out_specs, check_vma=False)
```

profile of v0, /device:TPU:0, one launch (start us, length us, event | category | flops | bytes accessed | tf_op | source)
XLA Modules:
  0.0 1260.5 jit_solution(11902922079995836065)
XLA Ops:
  44.9 6.5 fusion.57
  70.5 4.3 collective-permute-start.5
  93.8 5.5 convert_reduce_fusion
  122.5 4.2 fusion.76
  126.7 7.2 reshape_stack.12
  134.6 6.5 fusion.125
  141.1 9.2 reshape_stack.14
  150.4 6.8 fusion.66
  157.2 9.3 reshape_stack.15
  166.6 42.8 %reduce-scatter.10.cloned.1.call-done = f32[8,2304]{1,0:T(8,128)} async-done(((f32[8,73728]{1,0:T(8,128)}), f32[8,2304]{1,0:T(8,128)}) %reduce-scatter.10.cloned.1.call-update) | async-done | bytes 73744 | tf_op jit(solution)/shard_map/reduce_scatter | solution.py:342
  211.0 123.2 %reduce-scatter.8.cloned.1.call-done = f32[8,6912]{1,0:T(8,128)} async-done(((f32[8,221184]{1,0:T(8,128)}), f32[8,6912]{1,0:T(8,128)}) %reduce-scatter.8.cloned.1.call-update) | async-done | bytes 221200 | tf_op jit(solution)/shard_map/reduce_scatter | solution.py:341
  335.8 139.6 %reduce-scatter.12.cloned.1.call-done = f32[8,9216]{1,0:T(8,128)} async-done(((f32[8,294912]{1,0:T(8,128)}), f32[8,9216]{1,0:T(8,128)}) %reduce-scatter.12.cloned.1.call-update) | async-done | bytes 294928 | tf_op jit(solution)/shard_map/reduce_scatter | solution.py:343
  477.1 139.7 %reduce-scatter.14.cloned.1.call-done = f32[8,9216]{1,0:T(8,128)} async-done(((f32[8,294912]{1,0:T(8,128)}), f32[8,9216]{1,0:T(8,128)}) %reduce-scatter.14.cloned.1.call-update) | async-done | bytes 294928 | tf_op jit(solution)/shard_map/reduce_scatter | solution.py:344
  630.6 3.6 all-reduce.2
  639.2 41.3 %all-reduce = (f32[1,768]{1,0:T(1,128)}, f32[1,768]{1,0:T(1,128)}, f32[1,768]{1,0:T(1,128)}, f32[1,768]{1,0:T(1,128)}, f32[1,3072]{1,0:T(1,128)}, /*index=5*/f32[96]{0:T(128)}) all-reduce(f32[1,768]{1,0:T(1,128)S(1)} %stack.15, f32[1,768]{1,0:T(1,128)S(1)} %stack.16, ...), channel_id=1, replica_groups=mesh['dp'=16,'seq'=2] {'dp','seq'}, use_global_device_ids=true, to_apply=%region_26.27 | all-reduce | flops 6240 | bytes 49920 | tf_op jit(solution)/shard_map/psum | solution.py:323
  683.6 51.8 %all-gather.5.cloned.1.call-done = bf16[8,221184]{1,0:T(8,128)(2,1)} async-done(((bf16[8,6912]{1,0:T(8,128)(2,1)}), bf16[8,221184]{1,0:T(8,128)(2,1)}) %all-gather.5.cloned.1.call-update) | async-done | bytes 3538960 | tf_op jit(solution)/shard_map/all_gather | solution.py:347
  735.4 6.3 reshape.958
  741.8 59.6 %all-gather.9.cloned.1.call-done = bf16[8,294912]{1,0:T(8,128)(2,1)} async-done(((bf16[8,9216]{1,0:T(8,128)(2,1)}), bf16[8,294912]{1,0:T(8,128)(2,1)}) %all-gather.9.cloned.1.call-update) | async-done | bytes 4718608 | tf_op jit(solution)/shard_map/all_gather | solution.py:353
  801.4 7.9 reshape.962
  809.3 57.4 %all-gather.11.cloned.1.call-done = bf16[8,294912]{1,0:T(8,128)(2,1)} async-done(((bf16[8,9216]{1,0:T(8,128)(2,1)}), bf16[8,294912]{1,0:T(8,128)(2,1)}) %all-gather.11.cloned.1.call-update) | async-done | bytes 4718608 | tf_op jit(solution)/shard_map/all_gather | solution.py:356
  866.7 7.9 reshape.964
  874.6 123.7 %all-reduce.8.cloned.1.call-done = (f32[48,768]{1,0:T(8,128)}, f32[768,96]{0,1:T(8,128)}) async-done(((f32[48,768]{1,0:T(8,128)}, f32[768,96]{0,1:T(8,128)}), (f32[48,768]{1,0:T(8,128)}, f32[768,96]{0,1:T(8,128)})) %all-reduce.8.cloned.1.call-update) | async-done | bytes 442384 | tf_op jit(solution)/shard_map/psum | solution.py:323
  998.3 115.3 %all-reduce.6.cloned.1.call-done = f32[128,768]{1,0:T(8,128)} async-done(((f32[128,768]{1,0:T(8,128)}), f32[128,768]{1,0:T(8,128)}) %all-reduce.6.cloned.1.call-update) | async-done | bytes 393232 | tf_op jit(solution)/shard_map/psum | solution.py:313
  1113.7 135.2 %reduce-scatter.6.cloned.1.call-done = f32[64,768]{1,0:T(8,128)} async-done(((f32[1024,768]{1,0:T(8,128)}), f32[64,768]{1,0:T(8,128)}) %reduce-scatter.6.cloned.1.call-update) | async-done | bytes 196624 | tf_op jit(solution)/shard_map/reduce_scatter | solution.py:312
  (260 shorter events, 128.6 us)
Async XLA Ops:
  7.2 202.2 %reduce-scatter.10.cloned.1.call-start = ((), (), s32[]{:S(2)}) async-start(), calls=%async_computation.9 | async-start | bytes 2433024 | tf_op jit(solution)/shard_map/reduce_scatter | solution.py:342
  12.5 50.5 %copy-start.32 = (f32[768]{0:T(1024)}, f32[768]{0:T(1024)S(1)}, u32[]{:S(2)}) copy-start(f32[768]{0:T(1024)S(1)} %get-tuple-element.71) | copy-start | bytes 9220
  14.1 15.5 %collective-permute-start.2 = (bf16[1,128,768]{2,1,0:T(8,128)(2,1)}, bf16[1,128,768]{2,1,0:T(8,128)(2,1)}, u32[]{:S(2)}, u32[]{:S(2)}) collective-permute-start(bf16[1,128,768]{2,1,0:T(8,128)(2,1)} %get-tuple-element.46), channel_id=1, source_target_pairs={{0,1},{2,3},{4,5},{6,7},{8,9},{10,11},{12,13},{14,15},{16,17},{18,... | collective-permute-start | bytes 589832 | tf_op jit(solution)/shard_map/ppermute | solution.py:14
  17.6 9.9 collective-permute-start.1
  19.5 17.6 %collective-permute-start = (bf16[1,128,768]{2,1,0:T(8,128)(2,1)}, bf16[1,128,768]{2,1,0:T(8,128)(2,1)}, u32[]{:S(2)}, u32[]{:S(2)}) collective-permute-start(bf16[1,128,768]{2,1,0:T(8,128)(2,1)} %get-tuple-element.48), channel_id=1, source_target_pairs={{0,1},{2,3},{4,5},{6,7},{8,9},{10,11},{12,13},{14,15},{16,17},{18,... | collective-permute-start | bytes 589832 | tf_op jit(solution)/shard_map/ppermute | solution.py:14
  23.3 21.6 %copy-start.34 = (f32[768]{0:T(1024)}, f32[768]{0:T(1024)S(1)}, u32[]{:S(2)}) copy-start(f32[768]{0:T(1024)S(1)} %get-tuple-element.73) | copy-start | bytes 9220
  53.3 2.1 collective-permute-start.3
  64.6 12.2 collective-permute-start.6
  67.5 7.3 collective-permute-start.4
  70.5 13.3 %collective-permute-start.5 = (bf16[1,128,768]{2,1,0:T(8,128)(2,1)}, bf16[1,128,768]{2,1,0:T(8,128)(2,1)}, u32[]{:S(2)}, u32[]{:S(2)}) collective-permute-start(bf16[1,128,768]{2,1,0:T(8,128)(2,1)} %get-tuple-element.45), channel_id=1, source_target_pairs={{0,1},{2,3},{4,5},{6,7},{8,9},{10,11},{12,13},{14,15},{16,17},{18,... | collective-permute-start | bytes 589832 | tf_op jit(solution)/shard_map/ppermute | solution.py:14
  108.1 226.0 %reduce-scatter.8.cloned.1.call-start = ((), (), s32[]{:S(2)}) async-start(), calls=%async_computation.7 | async-start | bytes 7299072 | tf_op jit(solution)/shard_map/reduce_scatter | solution.py:341
  116.3 3.9 collective-permute-start.7
  118.3 3.5 collective-permute-start.8
  133.9 341.5 %reduce-scatter.12.cloned.1.call-start = ((), (), s32[]{:S(2)}) async-start(), calls=%async_computation.11 | async-start | bytes 9732096 | tf_op jit(solution)/shard_map/reduce_scatter | solution.py:343
  150.4 466.4 %reduce-scatter.14.cloned.1.call-start = ((), (), s32[]{:S(2)}) async-start(), calls=%async_computation.13 | async-start | bytes 9732096 | tf_op jit(solution)/shard_map/reduce_scatter | solution.py:344
  166.5 453.9 %copy-start.45 = (f32[128]{0:T(128)S(1)}, f32[128]{0:T(128)}, u32[]{:S(2)}) copy-start(f32[128]{0:T(128)} %copy-done.43) | copy-start | bytes 1540
  166.5 453.9 %copy-start.49 = (f32[128]{0:T(128)S(1)}, f32[128]{0:T(128)}, u32[]{:S(2)}) copy-start(f32[128]{0:T(128)} %copy-done.47) | copy-start | bytes 1540
  166.6 513.9 %all-gather.7.cloned.1.call-start = ((), (), s32[]{:S(2)}) async-start(), calls=%async_computation.10 | async-start | bytes 1216512 | tf_op jit(solution)/shard_map/all_gather | solution.py:350
  210.9 524.5 %all-gather.5.cloned.1.call-start = ((), (), s32[]{:S(2)}) async-start(), calls=%async_computation.8 | async-start | bytes 3649536 | tf_op jit(solution)/shard_map/all_gather | solution.py:347
  335.8 465.6 %all-gather.9.cloned.1.call-start = ((), (), s32[]{:S(2)}) async-start(), calls=%async_computation.12 | async-start | bytes 4866048 | tf_op jit(solution)/shard_map/all_gather | solution.py:353
  477.1 389.6 %all-gather.11.cloned.1.call-start = ((), (), s32[]{:S(2)}) async-start(), calls=%async_computation.14 | async-start | bytes 4866048 | tf_op jit(solution)/shard_map/all_gather | solution.py:356
  618.5 379.9 %all-reduce.8.cloned.1.call-start = ((), (), s32[]{:S(2)}) async-start(), calls=%async_computation.15 | async-start | bytes 884736 | tf_op jit(solution)/shard_map/psum | solution.py:323
  628.7 485.0 %all-reduce.6.cloned.1.call-start = ((), (), s32[]{:S(2)}) async-start(), calls=%async_computation.5 | async-start | bytes 786432 | tf_op jit(solution)/shard_map/psum | solution.py:313
  629.2 619.7 %reduce-scatter.6.cloned.1.call-start = ((), (), s32[]{:S(2)}) async-start(), calls=%async_computation.6 | async-start | bytes 3342336 | tf_op jit(solution)/shard_map/reduce_scatter | solution.py:312
  (54 other events, 169.4 us)
Sparse Core Ops, SparseCore 0:
  108.3 101.0 reduce-scatter.9
  216.0 118.1 reduce-scatter.7
  340.6 134.7 reduce-scatter.11
  482.2 134.5 reduce-scatter.13
  619.6 53.5 all-gather.6
  676.5 58.9 all-gather.4
  738.9 62.4 all-gather.8
  804.3 62.4 all-gather.10
  873.2 125.0 all-reduce.7
  1004.8 108.8 all-reduce.5
  1119.2 129.6 reduce-scatter.5
where the time goes:
time: 1260 us
  waiting for transfers between devices  991 us (79%)
  local copies, waits for them, and re-layouts  84.4 us (7%)
  matrix products  68.3 us (5%)
  blocking collectives  44.9 us (4%)
  other arithmetic  34.9 us (3%)
  starting transfers between devices  20.1 us (2%)
  between operations  17 us (1%)
    reduce_scatter x1, waiting for transfers between devices, local(): lax.psum_scatter(eight_rows(down_stack), ('dp', 'seq'), scatter_dimension...  140 us
    reduce_scatter x1, waiting for transfers between devices, local(): lax.psum_scatter(eight_rows(up_stack), ('dp', 'seq'), scatter_dimension=1...  140 us
    reduce_scatter x1, waiting for transfers between devices, local(): lax.psum_scatter(class_term, 'dp', scatter_dimension=0, tiled=True)  135 us
    psum x1, waiting for transfers between devices, local(): lax.psum((patch_grad_part, head_weight_grad, head_bias_grad, jnp.stack(gr...  124 us
    reduce_scatter x1, waiting for transfers between devices, local(): lax.psum_scatter(eight_rows(qkv_stack), ('dp', 'seq'), scatter_dimension=...  123 us
    psum x1, waiting for transfers between devices, local(): pos_grad = lax.psum(pos_part, 'dp')  115 us
    all_gather x1, waiting for transfers between devices, local(): lax.all_gather(flat_parts[2].astype(jnp.bfloat16), ('dp', 'seq'), axis=1,...  59.6 us
    all_gather x1, waiting for transfers between devices, local(): lax.all_gather(flat_parts[3].astype(jnp.bfloat16), ('dp', 'seq'), axis=1,...  57.4 us
  transfers between devices with their start and end apart: 20, of which 12 were waited for; matrix products, arithmetic and copies ran while one was open for 10% of the time, Pallas kernels for 0%

commit v1 on v0

--- a/solution.py
+++ b/solution.py
@@ -1,3 +1,4 @@
+import functools
 import jax
 import jax.numpy as jnp
 from jax import lax
@@ -6,6 +7,13 @@
 HEAD_DIM = 64
 precise = lax.Precision.HIGHEST
 norm_eps = 1e-05
+
+
+def process_tables_by_axis(point, row_axis, device_axis):
+    return lax.psum(lax.psum(point, row_axis), device_axis)
+
+
+roots_show = functools.partial(process_tables_by_axis, row_axis="seq", device_axis="dp")
 
 
 def shifted_2(shard, axis, by):
@@ -320,7 +328,7 @@
         ln2_gain_grad,
         ln2_bias_grad,
         up_bias_grad,
-    ) = lax.psum(
+    ) = roots_show(
         (
             patch_grad_part,
             head_weight_grad,
@@ -330,8 +338,7 @@
             jnp.stack(grads_g2),
             jnp.stack(grads_b2),
             jnp.stack(grads_ub),
-        ),
-        ("dp", "seq"),
+        )
     )
     qkv_stack = jnp.stack(grads_qkv)
     out_stack = jnp.stack(grads_out)

time: 1260 us -> 916 us (0.73)
  waiting for transfers between devices: 991 us -> 604 us
  blocking collectives: 44.9 us -> 80.6 us
    psum x2, waiting for transfers between devices: 239 us -> 0.01 us  [process_tables_by_axis(): return lax.psum(lax.psum(point, row_axis), device_axis)]
    reduce_scatter x1, waiting for transfers between devices: 135 us -> 15.5 us  [local(): lax.psum_scatter(class_term, 'dp', scatter_dimension=0, tiled=True)]
    psum x1, blocking collectives: 41.3 us -> 75.4 us  [process_tables_by_axis(): return lax.psum(lax.psum(point, row_axis), device_axis)]
    all_gather x1, waiting for transfers between devices: 51.8 us -> 25.6 us  [local(): lax.all_gather(flat_parts[0].astype(jnp.bfloat16), ('dp', 'seq'), axis=1,...]
  transfers between devices with their start and end apart: 20 -> 20, of which waited for: 12 -> 10; matrix products, arithmetic and copies ran while one was open for 10% -> 14% of each run, Pallas kernels for 0% -> 0%
where the time goes in v1:
time: 916 us; the launch traced here: 914 us
  waiting for transfers between devices  604 us (66%)
  local copies, waits for them, and re-layouts  88.4 us (10%)
  blocking collectives  80.6 us (9%)
  matrix products  67.3 us (7%)
  other arithmetic  34.9 us (4%)
  starting transfers between devices  20 us (2%)
  between operations  18.9 us (2%)
    reduce_scatter x1, waiting for transfers between devices, local(): lax.psum_scatter(eight_rows(up_stack), ('dp', 'seq'), scatter_dimension=1...  140 us
    reduce_scatter x1, waiting for transfers between devices, local(): lax.psum_scatter(eight_rows(down_stack), ('dp', 'seq'), scatter_dimension...  139 us
    reduce_scatter x1, waiting for transfers between devices, local(): lax.psum_scatter(eight_rows(qkv_stack), ('dp', 'seq'), scatter_dimension=...  123 us
    psum x1, blocking collectives, process_tables_by_axis(): return lax.psum(lax.psum(point, row_axis), device_axis)  75.4 us
    all_gather x1, waiting for transfers between devices, local(): lax.all_gather(flat_parts[2].astype(jnp.bfloat16), ('dp', 'seq'), axis=1,...  62.3 us
    all_gather x1, waiting for transfers between devices, local(): lax.all_gather(flat_parts[3].astype(jnp.bfloat16), ('dp', 'seq'), axis=1,...  59.9 us
    reduce_scatter x1, waiting for transfers between devices, local(): lax.psum_scatter(eight_rows(out_stack), ('dp', 'seq'), scatter_dimension=...  35.4 us
    another operation x4, local copies, waits for them, and re-layouts, eight_rows(): return matrix.reshape(8, -1)  29.2 us
  transfers between devices with their start and end apart: 20, of which 10 were waited for; matrix products, arithmetic and copies ran while one was open for 14% of the time, Pallas kernels for 0%

profile of v1, /device:TPU:0, one launch (start us, length us, event | category | flops | bytes accessed | tf_op | source)
XLA Modules:
  0.0 913.6 jit_solution(12029548943059434236)
XLA Ops:
  45.6 6.5 fusion.57
  71.3 4.3 collective-permute-start.5
  94.5 5.5 convert_reduce_fusion
  105.4 3.5 reshape_stack.13
  123.3 4.2 fusion.76
  127.5 7.2 reshape_stack.12
  135.4 6.5 fusion.125
  141.9 9.2 %reshape_stack.14 = f32[8,294912]{1,0:T(8,128)} reshape(f32[768,3072]{1,0:T(8,128)} %fusion.125) | data formatting | bytes 18874368 | tf_op jit(solution)/shard_map/reshape;stack | solution.py:53
  151.2 6.8 fusion.66
  158.0 9.3 %reshape_stack.15 = f32[8,294912]{1,0:T(8,128)} reshape(f32[3072,768]{1,0:T(8,128)} %fusion.66) | data formatting | bytes 18874368 | tf_op jit(solution)/shard_map/reshape;stack | solution.py:53
  169.3 3.4 multiply_reduce_fusion.2
  174.7 35.4 %reduce-scatter.10.cloned.1.call-done = f32[8,2304]{1,0:T(8,128)} async-done(((f32[8,73728]{1,0:T(8,128)}), f32[8,2304]{1,0:T(8,128)}) %reduce-scatter.10.cloned.1.call-update) | async-done | bytes 73744 | tf_op jit(solution)/shard_map/reduce_scatter | solution.py:349
  211.7 123.2 %reduce-scatter.8.cloned.1.call-done = f32[8,6912]{1,0:T(8,128)} async-done(((f32[8,221184]{1,0:T(8,128)}), f32[8,6912]{1,0:T(8,128)}) %reduce-scatter.8.cloned.1.call-update) | async-done | bytes 221200 | tf_op jit(solution)/shard_map/reduce_scatter | solution.py:348
  336.6 139.7 %reduce-scatter.12.cloned.1.call-done = f32[8,9216]{1,0:T(8,128)} async-done(((f32[8,294912]{1,0:T(8,128)}), f32[8,9216]{1,0:T(8,128)}) %reduce-scatter.12.cloned.1.call-update) | async-done | bytes 294928 | tf_op jit(solution)/shard_map/reduce_scatter | solution.py:350
  478.1 139.5 %reduce-scatter.14.cloned.1.call-done = f32[8,9216]{1,0:T(8,128)} async-done(((f32[8,294912]{1,0:T(8,128)}), f32[8,9216]{1,0:T(8,128)}) %reduce-scatter.14.cloned.1.call-update) | async-done | bytes 294928 | tf_op jit(solution)/shard_map/reduce_scatter | solution.py:351
  628.4 5.2 all-reduce.2
  636.9 75.4 %all-reduce = (f32[1,768]{1,0:T(1,128)}, f32[1,768]{1,0:T(1,128)}, f32[1,768]{1,0:T(1,128)}, f32[1,768]{1,0:T(1,128)}, f32[1,3072]{1,0:T(1,128)}, /*index=5*/f32[96]{0:T(128)}) all-reduce(f32[1,768]{1,0:T(1,128)S(1)} %copy-done.55, f32[1,768]{1,0:T(1,128)} %get-tuple-element.37, ...), channel_id=1, replica_groups=mesh['dp'=16,'seq'=2] {'dp'}, use_global_device_ids=true, to_apply=%region_28.29 | all-reduce | flops 6240 | bytes 49920 | tf_op jit(solution)/shard_map/psum | solution.py:13
  715.4 25.6 %all-gather.5.cloned.1.call-done = bf16[8,221184]{1,0:T(8,128)(2,1)} async-done(((bf16[8,6912]{1,0:T(8,128)(2,1)}), bf16[8,221184]{1,0:T(8,128)(2,1)}) %all-gather.5.cloned.1.call-update) | async-done | bytes 3538960 | tf_op jit(solution)/shard_map/all_gather | solution.py:354
  741.1 6.3 reshape.958
  747.4 62.3 %all-gather.9.cloned.1.call-done = bf16[8,294912]{1,0:T(8,128)(2,1)} async-done(((bf16[8,9216]{1,0:T(8,128)(2,1)}), bf16[8,294912]{1,0:T(8,128)(2,1)}) %all-gather.9.cloned.1.call-update) | async-done | bytes 4718608 | tf_op jit(solution)/shard_map/all_gather | solution.py:360
  809.6 7.9 reshape.962
  817.6 59.9 %all-gather.11.cloned.1.call-done = bf16[8,294912]{1,0:T(8,128)(2,1)} async-done(((bf16[8,9216]{1,0:T(8,128)(2,1)}), bf16[8,294912]{1,0:T(8,128)(2,1)}) %all-gather.11.cloned.1.call-update) | async-done | bytes 4718608 | tf_op jit(solution)/shard_map/all_gather | solution.py:363
  877.5 8.0 reshape.964
  885.5 15.5 %reduce-scatter.6.cloned.1.call-done = f32[64,768]{1,0:T(8,128)} async-done(((f32[1024,768]{1,0:T(8,128)}), f32[64,768]{1,0:T(8,128)}) %reduce-scatter.6.cloned.1.call-update) | async-done | bytes 196624 | tf_op jit(solution)/shard_map/reduce_scatter | solution.py:320
  (268 shorter events, 124.5 us)
Async XLA Ops:
  8.1 202.1 %reduce-scatter.10.cloned.1.call-start = ((), (), s32[]{:S(2)}) async-start(), calls=%async_computation.8 | async-start | bytes 2433024 | tf_op jit(solution)/shard_map/reduce_scatter | solution.py:349
  13.4 50.5 %copy-start.34 = (f32[768]{0:T(1024)}, f32[768]{0:T(1024)S(1)}, u32[]{:S(2)}) copy-start(f32[768]{0:T(1024)S(1)} %get-tuple-element.80) | copy-start | bytes 9220
  14.9 15.4 %collective-permute-start.2 = (bf16[1,128,768]{2,1,0:T(8,128)(2,1)}, bf16[1,128,768]{2,1,0:T(8,128)(2,1)}, u32[]{:S(2)}, u32[]{:S(2)}) collective-permute-start(bf16[1,128,768]{2,1,0:T(8,128)(2,1)} %get-tuple-element.55), channel_id=1, source_target_pairs={{0,1},{2,3},{4,5},{6,7},{8,9},{10,11},{12,13},{14,15},{16,17},{18,... | collective-permute-start | bytes 589832 | tf_op jit(solution)/shard_map/ppermute | solution.py:22
  18.5 9.8 %collective-permute-start.1 = (bf16[1,128]{1,0:T(2,128)(2,1)}, bf16[1,128]{1,0:T(2,128)(2,1)}, u32[]{:S(2)}, u32[]{:S(2)}) collective-permute-start(bf16[1,128]{1,0:T(2,128)(2,1)} %get-tuple-element.61), channel_id=1, source_target_pairs={{0,1},{2,3},{4,5},{6,7},{8,9},{10,11},{12,13},{14,15},{16,17},{18,... | collective-permute-start | bytes 776 | tf_op jit(solution)/shard_map/ppermute | solution.py:22
  20.3 17.6 %collective-permute-start = (bf16[1,128,768]{2,1,0:T(8,128)(2,1)}, bf16[1,128,768]{2,1,0:T(8,128)(2,1)}, u32[]{:S(2)}, u32[]{:S(2)}) collective-permute-start(bf16[1,128,768]{2,1,0:T(8,128)(2,1)} %get-tuple-element.57), channel_id=1, source_target_pairs={{0,1},{2,3},{4,5},{6,7},{8,9},{10,11},{12,13},{14,15},{16,17},{18,... | collective-permute-start | bytes 589832 | tf_op jit(solution)/shard_map/ppermute | solution.py:22
  24.0 21.6 %copy-start.36 = (f32[768]{0:T(1024)}, f32[768]{0:T(1024)S(1)}, u32[]{:S(2)}) copy-start(f32[768]{0:T(1024)S(1)} %get-tuple-element.82) | copy-start | bytes 9220
  54.1 2.1 collective-permute-start.3
  65.4 12.2 %collective-permute-start.6 = (bf16[1,128,768]{2,1,0:T(8,128)(2,1)}, bf16[1,128,768]{2,1,0:T(8,128)(2,1)}, u32[]{:S(2)}, u32[]{:S(2)}) collective-permute-start(bf16[1,128,768]{2,1,0:T(8,128)(2,1)} %get-tuple-element.52), channel_id=1, source_target_pairs={{0,1},{2,3},{4,5},{6,7},{8,9},{10,11},{12,13},{14,15},{16,17},{18,... | collective-permute-start | bytes 589832 | tf_op jit(solution)/shard_map/ppermute | solution.py:22
  68.3 7.3 collective-permute-start.4
  71.3 13.3 %collective-permute-start.5 = (bf16[1,128,768]{2,1,0:T(8,128)(2,1)}, bf16[1,128,768]{2,1,0:T(8,128)(2,1)}, u32[]{:S(2)}, u32[]{:S(2)}) collective-permute-start(bf16[1,128,768]{2,1,0:T(8,128)(2,1)} %get-tuple-element.54), channel_id=1, source_target_pairs={{0,1},{2,3},{4,5},{6,7},{8,9},{10,11},{12,13},{14,15},{16,17},{18,... | collective-permute-start | bytes 589832 | tf_op jit(solution)/shard_map/ppermute | solution.py:22
  108.9 226.1 %reduce-scatter.8.cloned.1.call-start = ((), (), s32[]{:S(2)}) async-start(), calls=%async_computation.6 | async-start | bytes 7299072 | tf_op jit(solution)/shard_map/reduce_scatter | solution.py:348
  117.1 3.9 collective-permute-start.7
  119.1 3.5 collective-permute-start.8
  134.7 341.7 %reduce-scatter.12.cloned.1.call-start = ((), (), s32[]{:S(2)}) async-start(), calls=%async_computation.10 | async-start | bytes 9732096 | tf_op jit(solution)/shard_map/reduce_scatter | solution.py:350
  151.1 466.4 %reduce-scatter.14.cloned.1.call-start = ((), (), s32[]{:S(2)}) async-start(), calls=%async_computation.12 | async-start | bytes 9732096 | tf_op jit(solution)/shard_map/reduce_scatter | solution.py:351
  167.3 453.7 %all-reduce.9.cloned.1.call-start = ((), (), s32[]{:S(2)}) async-start(), calls=%async_computation.15 | async-start | bytes 884736 | tf_op jit(solution)/shard_map/psum | solution.py:13
  174.7 537.6 %all-gather.7.cloned.1.call-start = ((), (), s32[]{:S(2)}) async-start(), calls=%async_computation.9 | async-start | bytes 1216512 | tf_op jit(solution)/shard_map/all_gather | solution.py:357
  211.7 414.2 %copy-start.44 = (f32[768]{0:T(1024)S(1)}, f32[768]{0:T(1024)}, u32[]{:S(2)}) copy-start(f32[768]{0:T(1024)} %get-tuple-element.19) | copy-start | bytes 9220
  211.7 414.8 %copy-start.43 = (f32[768]{0:T(1024)S(1)}, f32[768]{0:T(1024)}, u32[]{:S(2)}) copy-start(f32[768]{0:T(1024)} %get-tuple-element.23) | copy-start | bytes 9220
  211.7 529.4 %all-gather.5.cloned.1.call-start = ((), (), s32[]{:S(2)}) async-start(), calls=%async_computation.7 | async-start | bytes 3649536 | tf_op jit(solution)/shard_map/all_gather | solution.py:354
  336.6 473.1 %all-gather.9.cloned.1.call-start = ((), (), s32[]{:S(2)}) async-start(), calls=%async_computation.11 | async-start | bytes 4866048 | tf_op jit(solution)/shard_map/all_gather | solution.py:360
  478.0 399.5 %all-gather.11.cloned.1.call-start = ((), (), s32[]{:S(2)}) async-start(), calls=%async_computation.13 | async-start | bytes 4866048 | tf_op jit(solution)/shard_map/all_gather | solution.py:363
  621.0 264.4 %all-reduce.7.cloned.1.call-start = ((), (), s32[]{:S(2)}) async-start(), calls=%async_computation.14 | async-start | bytes 1671168 | tf_op jit(solution)/shard_map/psum | solution.py:13
  621.6 279.4 %reduce-scatter.6.cloned.1.call-start = ((), (), s32[]{:S(2)}) async-start(), calls=%async_computation.5 | async-start | bytes 3342336 | tf_op jit(solution)/shard_map/reduce_scatter | solution.py:320
  (58 other events, 172.2 us)
Sparse Core Ops, SparseCore 0:
  109.0 101.0 reduce-scatter.9
  216.8 118.1 reduce-scatter.7
  341.4 134.8 reduce-scatter.11
  483.1 134.3 reduce-scatter.13
  620.8 55.5 all-gather.6
  679.8 61.2 all-gather.4
  744.5 65.0 all-gather.8
  812.5 64.8 all-gather.10
Sparse Core Ops, SparseCore 1:
  174.8 20.1 all-reduce.8
  628.7 115.1 all-reduce.6
  749.3 151.7 reduce-scatter.5
